TPU v7x, 128 devices: a whole 4x4x4 slice. The times are simulated.
128 devices in a mesh: dp: 4 (over x), expert: 32 (over y, z, core).
Axes of the slice: x: 4, y: 4, z: 4, core: 2. Of those that a mesh axis runs over, the one named last changes fastest.
Arguments:
- tokens: bfloat16 [4096, 3584], P(('dp', 'expert')), may hold values from -6 to 6
- expert_ids: int32 [4096, 8], P(('dp', 'expert')), may hold values from 0 to 31, all different within a row; in each aligned block of 32 rows (0 to 31, 32 to 63, ...) at most 12 rows name the same one
- route_weights: float32 [4096, 8], P(('dp', 'expert')), may hold values from 0.1 to 1
- out_grad: bfloat16 [4096, 3584], P(('dp', 'expert')), may hold values from -6 to 6
- gate_weight: bfloat16 [32, 3584, 1024], P('expert', 'dp'), may hold values from -0.09375 to 0.09375
- up_weight: bfloat16 [32, 3584, 1024], P('expert', 'dp'), may hold values from -0.09375 to 0.09375
- down_weight: bfloat16 [32, 1024, 3584], P('expert', None, 'dp'), may hold values from -0.1875 to 0.1875
Outputs:
- mixed: bfloat16 [4096, 3584], P(('dp', 'expert'))
- tokens_grad: bfloat16 [4096, 3584], P(('dp', 'expert'))
- route_grad: float32 [4096, 8], P(('dp', 'expert'))
- gate_grad: bfloat16 [32, 3584, 1024], P('expert', 'dp')
- up_grad: bfloat16 [32, 3584, 1024], P('expert', 'dp')
- down_grad: bfloat16 [32, 1024, 3584], P('expert', None, 'dp')
Inputs may be any that keep to these rules, and one draw needn't show every extreme that they name: `expert_ids`: each row names 8 different experts; in each aligned block of 32 rows (the rows of one device) no expert is named by more than 12 rows, a bound that some block reaches.
All inputs are finite; a program needn't handle non-finite values.
Results may differ from a plain program's by a relative error of at most 0.0065.
Values may be sent and summed in bfloat16 or wider, within the bound.
A program may use at most 192 MiB of HBM per device.

v0:
```python
import jax
import jax.numpy as jnp
from jax import lax
from jax.sharding import PartitionSpec as P

BF = jnp.bfloat16
F32 = jnp.float32
LANES = 128


def dot32(a, b, dims):
    return lax.dot_general(a, b, (dims, ((), ())), preferred_element_type=F32)


def route_table(ids, weights, experts):
    onehot = (ids[:, :, None] == jnp.arange(experts, dtype=jnp.int32)).astype(jnp.int32)
    chosen = jnp.sum(onehot, axis=1)
    place = jnp.cumsum(chosen, axis=0) * chosen
    dense = jnp.sum(onehot.astype(F32) * weights[:, :, None], axis=1)
    high = lax.reduce_precision(dense, 8, 7)
    middle = lax.reduce_precision(dense - high, 8, 7)
    low = dense - high - middle
    return jnp.concatenate([place.astype(F32), high, middle, low], axis=1).astype(BF)


def to_slices(array, n_dp):
    rows, width = array.shape
    return lax.all_to_all(array, "dp", split_axis=1, concat_axis=0, tiled=True)


def dispatch(tokens, out_grad, table):
    n_dp = lax.axis_size("dp")
    tok = to_slices(tokens, n_dp)
    grad = to_slices(out_grad, n_dp)
    tab = lax.all_gather(table, "dp", axis=0, tiled=True)
    whole = lax.all_gather(jnp.concatenate([tok, grad, tab], axis=1), "expert", axis=0, tiled=False)
    return (whole, grad, tab)


def pick_rows(whole, slots, experts, n_dp, tok_rows, width):
    me = lax.axis_index("expert")
    tab = whole[:, :, 2 * width :].astype(F32)
    lane = jnp.arange(tab.shape[2], dtype=jnp.int32)
    place = jnp.sum(jnp.where(lane == me, tab, 0.0), axis=2)
    weight = jnp.sum(jnp.where((lane >= experts) & (lane % experts == me), tab, 0.0), axis=2)
    rows = n_dp * slots
    row = jnp.arange(rows, dtype=jnp.int32)
    tok = jnp.arange(n_dp * tok_rows, dtype=jnp.int32)
    same = row[:, None] // slots == tok[None, :] // tok_rows
    hit = same & (place[:, None, :] == (row % slots + 1).astype(F32)[None, :, None])
    picked = lax.dot_general(
        hit.astype(BF),
        whole[:, :, : 2 * width],
        (((2,), (1,)), ((0,), (0,))),
        preferred_element_type=F32,
    )
    scale = jnp.sum(jnp.where(hit, weight[:, None, :], 0.0), axis=2)
    x_rows = picked[:, :, :width].astype(BF).reshape(experts * rows, width)
    g_rows = (picked[:, :, width:] * scale[:, :, None]).astype(BF).reshape(experts * rows, width)
    return (x_rows, g_rows)


def activations(pre, quarter):
    gate, up, hgrad = (pre[:, i * quarter : (i + 1) * quarter].astype(F32) for i in range(3))
    sig = jax.nn.sigmoid(gate)
    act = gate * sig
    slope = sig * (1.0 + gate * (1.0 - sig))
    return jnp.concatenate(
        [(act * up).astype(BF), (hgrad * up * slope).astype(BF), (hgrad * act).astype(BF)], axis=1
    )


def combine(back, ids, grad, tab, slots, experts, n_dp, tok_rows, width):
    tab = tab.astype(F32)
    toks = n_dp * tok_rows
    place = tab[:, :experts]
    weight = (
        tab[:, experts : 2 * experts]
        + tab[:, 2 * experts : 3 * experts]
        + tab[:, 3 * experts : 4 * experts]
    )
    row = jnp.arange(n_dp * slots, dtype=jnp.int32)
    tok = jnp.arange(toks, dtype=jnp.int32)
    same = row[None, :] // slots == tok[:, None] // tok_rows
    hit = same[:, None, :] & (place[:, :, None] == (row % slots + 1).astype(F32))
    flat = hit.reshape(toks, -1)
    scaled = jnp.where(hit, weight[:, :, None], 0.0).reshape(toks, -1)
    out_rows = back[:, :width]
    in_rows = back[:, width:]
    mixed = lax.dot_general(
        scaled, out_rows.astype(F32), (((1,), (0,)), ((), ())), precision=lax.Precision.HIGHEST
    )
    tgrad = dot32(flat.astype(BF), in_rows, ((1,), (0,)))
    dots = dot32(grad, out_rows, ((1,), (1,)))
    route = jnp.sum(jnp.where(hit, dots.reshape(hit.shape), 0.0), axis=2)
    mixed = lax.all_to_all(mixed.astype(BF).reshape(n_dp, tok_rows, width), "dp", 0, 0, tiled=True)
    tgrad = lax.all_to_all(tgrad.astype(BF).reshape(n_dp, tok_rows, width), "dp", 0, 0, tiled=True)
    route = lax.psum_scatter(route, "dp", scatter_dimension=0, tiled=True)
    mixed = mixed.transpose(1, 0, 2).reshape(tok_rows, n_dp * width)
    tgrad = tgrad.transpose(1, 0, 2).reshape(tok_rows, n_dp * width)
    onehot = ids[:, :, None] == jnp.arange(experts, dtype=jnp.int32)
    route = jnp.sum(jnp.where(onehot, route[:, None, :], 0.0), axis=2)
    return (mixed, tgrad, route)


def per_device(tokens, ids, weights, out_grad, gate_weight, up_weight, down_weight):
    experts = lax.axis_size("expert")
    n_dp = lax.axis_size("dp")
    tok_rows, model = tokens.shape
    width = model // n_dp
    hidden = gate_weight.shape[2]
    quarter = hidden // n_dp
    slots = min(tok_rows, 3 * tok_rows * ids.shape[1] // (2 * experts))
    gate, up, down = (gate_weight[0], up_weight[0], down_weight[0])
    table = route_table(ids, weights, experts)
    whole, grad, tab = dispatch(tokens, out_grad, table)
    x_rows, g_rows = pick_rows(whole, slots, experts, n_dp, tok_rows, width)
    rows = x_rows.shape[0]
    part = jnp.stack(
        [
            dot32(x_rows, gate, ((1,), (0,))).astype(BF),
            dot32(x_rows, up, ((1,), (0,))).astype(BF),
            dot32(g_rows, down, ((1,), (1,))).astype(BF),
        ]
    )
    part = (
        part.reshape(3, rows, n_dp, quarter).transpose(2, 1, 0, 3).reshape(n_dp * rows, 3 * quarter)
    )
    pre = lax.psum_scatter(part, "dp", scatter_dimension=0, tiled=True)
    acts = activations(pre, quarter)
    terms = lax.all_gather(acts, "dp", axis=0, tiled=False)
    terms = terms.reshape(n_dp, rows, 3, quarter).transpose(2, 1, 0, 3).reshape(3, rows, hidden)
    hid, gterm, uterm = (terms[0], terms[1], terms[2])
    out_rows = dot32(hid, down, ((1,), (0,))).astype(BF)
    in_rows = (dot32(gterm, gate, ((1,), (1,))) + dot32(uterm, up, ((1,), (1,)))).astype(BF)
    send = jnp.concatenate([out_rows, in_rows], axis=1).reshape(experts, n_dp * slots, 2 * width)
    back = lax.all_to_all(send, "expert", split_axis=0, concat_axis=0, tiled=True)
    back = back.reshape(experts * n_dp * slots, 2 * width)
    gate_grad = dot32(x_rows, gterm, ((0,), (0,))).astype(BF)[None]
    up_grad = dot32(x_rows, uterm, ((0,), (0,))).astype(BF)[None]
    down_grad = dot32(hid, g_rows, ((0,), (0,))).astype(BF)[None]
    mixed, tgrad, route = combine(back, ids, grad, tab, slots, experts, n_dp, tok_rows, width)
    return (mixed, tgrad, route, gate_grad, up_grad, down_grad)


def solution(mesh):
    rows = P(("dp", "expert"), None)
    weights = (P("expert", "dp", None), P("expert", "dp", None), P("expert", None, "dp"))
    return jax.shard_map(
        per_device,
        mesh=mesh,
        in_specs=(rows, rows, rows, rows) + weights,
        out_specs=(rows, rows, rows) + weights,
        check_vma=False,
    )
```

profile of v0, /device:TPU:34, one launch (start us, length us, event | category | flops | bytes accessed | tf_op | source)
XLA Modules:
  0.0 510.5 jit_solution(16522338820058106155)
XLA Ops:
  7.2 1.8 copy.108
  9.0 4.8 all-to-all-start.1
  13.8 0.8 copy.82
  14.5 0.1 convert_reduce_fusion
  14.7 0.8 copy.83
  15.5 1.6 copy.109
  17.1 0.1 fusion.38
  17.3 1.5 all-to-all-done.1
  18.8 4.8 all-to-all-start
  23.7 0.1 pad_maximum_fusion.4
  23.7 11.9 %all_gather.15 = bf16[128,128]{1,0:T(8,128)(2,1)S(1)} all-gather(bf16[32,128]{1,0:T(8,128)(2,1)S(1)} %pad_maximum_fusion.4), channel_id=1, replica_groups=mesh['dp'=4,'expert'=32] {'dp'}, dimensions={0}, use_global_device_ids=true | all-gather | bytes 40960 | tf_op jit(solution)/shard_map/all_gather | solution.py:35
  35.7 0.8 pad_maximum_fusion.3
  36.6 0.1 broadcast_compare_fusion
  36.7 71.4 %all-gather.5.cloned.1.call-done = bf16[4096,1920]{1,0:T(8,128)(2,1)} async-done(((bf16[128,1920]{1,0:T(8,128)(2,1)}), bf16[4096,1920]{1,0:T(8,128)(2,1)}) %all-gather.5.cloned.1.call-update) | async-done | bytes 15728656 | tf_op jit(solution)/shard_map/all_gather | solution.py:36
  108.1 2.0 fusion.10
  110.1 6.4 %fusion = f32[32,48,1792]{2,1,0:T(8,128)S(1)} fusion(bf16[32,128,1920]{2,1,0:T(8,128)(2,1)} %bitcast.95, f32[32,128]{1,0:T(8,128)S(1)} %get-tuple-element.13, f32[48]{0:T(128)S(1)} %fusion.41, pred[48,128]{1,0:T(8,128)(4,1)S(1)} %broadcast_compare_fusion), kind=kOutput, calls=%fused_computation | convolution fusion | flops 705036288 | bytes 25712832 | tf_op jit(solution)/shard_map/dot_general | solution.py:51
  116.5 0.4 select_reduce_fusion.1
  116.9 0.3 slice.117
  117.2 0.4 fusion.2
  117.6 2.5 copy-done.9
  120.0 3.7 convolution_convert_fusion
  123.7 2.4 copy.90
  126.2 3.8 convolution_convert_fusion.2
  130.0 2.4 copy.88
  132.5 4.3 convolution_convert_fusion.1
  136.8 2.4 copy.89
  139.2 9.2 %pad_maximum_fusion = bf16[3,1536,4,256]{1,2,3,0:T(4,128)(2,1)} fusion(bf16[1,1536,4,256]{1,2,3,0:T(4,128)(2,1)S(1)} %copy.90, bf16[1,1536,4,256]{1,2,3,0:T(4,128)(2,1)S(1)} %copy.89, bf16[1,1536,4,256]{1,2,3,0:T(4,128)(2,1)S(1)} %copy.88), kind=kLoop, calls=%fused_computation.2 | loop fusion | flops 9437184 | bytes 18874368 | tf_op jit(solution)/shard_map/stack | solution.py:119
  148.4 10.3 %copy.105 = bf16[96,8,4,1536]{3,1,2,0:T(8,128)(2,1)} copy(bf16[96,8,4,1536]{3,2,1,0:T(4,128)(2,1)} %bitcast.98) | data formatting | bytes 18874368
  158.8 87.8 %reduce-scatter.5.cloned.1.call-done = bf16[1536,768]{0,1:T(8,128)(2,1)} async-done(((bf16[6144,768]{0,1:T(8,128)(2,1)}), bf16[1536,768]{0,1:T(8,128)(2,1)}) %reduce-scatter.5.cloned.1.call-update) | async-done | bytes 2359312 | tf_op jit(solution)/shard_map/reduce_scatter | solution.py:129
  246.7 2.6 fusion.18
  249.2 1.5 pad_maximum_fusion.2
  250.8 93.0 %all-gather.7.cloned.1.call-done = bf16[6144,768]{0,1:T(8,128)(2,1)} async-done(((bf16[1536,768]{0,1:T(8,128)(2,1)}), bf16[6144,768]{0,1:T(8,128)(2,1)}) %all-gather.7.cloned.1.call-update) | async-done | bytes 9437200 | tf_op jit(solution)/shard_map/all_gather | solution.py:131
  343.8 15.4 %reshape.277 = bf16[4,1536,3,256]{1,0,3,2:T(4,128)(2,1)} reshape(bf16[6144,768]{0,1:T(8,128)(2,1)} %all-gather.7.cloned.1.call-done) | data formatting | bytes 18874368 | tf_op jit(solution)/shard_map/reshape | solution.py:132
  359.3 6.0 %fusion.42 = (bf16[1,1536,4,256]{1,2,3,0:T(4,128)(2,1)S(1)}, bf16[1,1536,4,256]{1,2,3,0:T(4,128)(2,1)S(1)}, bf16[1,1536,4,256]{1,2,3,0:T(4,128)(2,1)S(1)}) fusion(bf16[3,1536,4,256]{1,2,3,0:T(4,128)(2,1)} %bitcast.97), kind=kLoop, calls=%fused_computation.93 | loop fusion | bytes 18874368 | tf_op jit(solution)/shard_map/slice | solution.py:133
  365.3 0.6 copy.92
  365.9 3.0 fusion.15
  368.9 0.6 copy.93
  369.5 0.6 copy.91
  370.1 2.3 copy-done.10
  372.3 3.3 convolution_convert_fusion.3
  375.7 3.3 add_convert_fusion
  379.0 2.8 pad_maximum_fusion.1
  381.8 8.1 %copy.94 = bf16[1536,1792]{1,0:T(8,128)(2,1)} copy(bf16[1536,1792]{0,1:T(8,128)(2,1)} %pad_maximum_fusion.1) | data formatting | bytes 11010048 | tf_op jit(solution)/shard_map/concatenate | solution.py:136
  389.9 7.5 %all-to-all-start.2 = ((bf16[32,48,1792]{2,1,0:T(8,128)(2,1)}), bf16[32,48,1792]{2,1,0:T(8,128)(2,1)}, u32[]{:S(2)}, u32[]{:S(2)}) async-start(bf16[32,48,1792]{2,1,0:T(8,128)(2,1)} %bitcast.99), calls=%async_computation.3 | async-start | bytes 11010048 | tf_op jit(solution)/shard_map/all_to_all | solution.py:137
  397.6 0.1 eq.122
  397.6 0.1 slice_add_fusion
  397.9 0.3 fusion.33
  398.2 0.3 bitcast_select_fusion
  398.5 7.5 %convert_bitcast_fusion = bf16[1,1024,896]{2,1,0:T(8,128)(2,1)} fusion(bf16[1536,1024]{0,1:T(8,128)(2,1)} %bitcast.105, bf16[1536,896]{1,0:T(8,128)(2,1)} %bitcast.114), kind=kOutput, calls=%fused_computation.36 | convolution fusion | flops 2819489792 | bytes 7733248 | tf_op jit(solution)/shard_map/dot_general | solution.py:12
  406.0 4.4 convert_bitcast_fusion.1
  410.4 61.9 %all-to-all-done.2 = bf16[32,48,1792]{2,1,0:T(8,128)(2,1)} async-done(((bf16[32,48,1792]{2,1,0:T(8,128)(2,1)}), bf16[32,48,1792]{2,1,0:T(8,128)(2,1)}, u32[]{:S(2)}, u32[]{:S(2)}) %all-to-all-start.2) | async-done | bytes 5505056 | tf_op jit(solution)/shard_map/all_to_all | solution.py:137
  472.3 2.6 fusion.5
  475.0 0.3 select_reduce_fusion
  475.2 0.7 copy.99
  476.0 3.1 fusion.30
  479.1 4.5 all-to-all-start.4
  483.6 4.0 fusion.27
  487.6 1.2 all-to-all-done.4
  488.8 4.9 all-to-all-start.3
  493.6 7.1 %convert_bitcast_fusion.2 = bf16[1,896,1024]{2,1,0:T(8,128)(2,1)} fusion(bf16[1536,896]{1,0:T(8,128)(2,1)} %bitcast.111, bf16[1536,1024]{0,1:T(8,128)(2,1)} %bitcast.101), kind=kOutput, calls=%fused_computation.38 | convolution fusion | flops 2819489792 | bytes 7733248 | tf_op jit(solution)/shard_map/dot_general | solution.py:12
  500.8 0.9 select_reduce_fusion.2
  501.7 0.7 copy.98
  502.3 0.7 copy.104
  503.0 0.7 copy.103
  (48 shorter events, 0.6 us)
Async XLA Ops:
  7.2 119.0 %copy-start = (bf16[1,896,1024]{2,1,0:T(8,128)(2,1)S(1)}, bf16[1,896,1024]{2,1,0:T(8,128)(2,1)}, u32[]{:S(2)}) copy-start(bf16[1,896,1024]{2,1,0:T(8,128)(2,1)} %param.11) | copy-start | bytes 5505028
  9.0 9.9 %all-to-all-start.1 = ((bf16[32,4,896]{2,0,1:T(8,128)(2,1)}), bf16[32,4,896]{2,0,1:T(8,128)(2,1)S(1)}, u32[]{:S(2)}, u32[]{:S(2)}) async-start(bf16[32,4,896]{2,0,1:T(8,128)(2,1)} %bitcast.92), calls=%async_computation.1 | async-start | bytes 458752 | tf_op jit(solution)/shard_map/all_to_all | solution.py:28
  18.8 16.8 %all-to-all-start = ((bf16[32,4,896]{2,0,1:T(8,128)(2,1)}), bf16[32,4,896]{2,0,1:T(8,128)(2,1)S(1)}, u32[]{:S(2)}, u32[]{:S(2)}) async-start(bf16[32,4,896]{2,0,1:T(8,128)(2,1)} %bitcast.93), calls=%async_computation | async-start | bytes 458752 | tf_op jit(solution)/shard_map/all_to_all | solution.py:28
  23.6 84.5 %all-gather.5.cloned.1.call-start = ((), (), s32[]{:S(2)}) async-start(), calls=%async_computation.8 | async-start | bytes 16220160 | tf_op jit(solution)/shard_map/all_gather | solution.py:36
  36.5 210.1 %reduce-scatter.5.cloned.1.call-start = ((), (), s32[]{:S(2)}) async-start(), calls=%async_computation.7 | async-start | bytes 11796480 | tf_op jit(solution)/shard_map/reduce_scatter | solution.py:129
  117.2 15.3 %copy-start.6 = (bf16[32,48,896]{2,1,0:T(8,128)(2,1)}, bf16[32,48,896]{2,1,0:T(8,128)(2,1)S(1)}, u32[]{:S(2)}) copy-start(bf16[32,48,896]{2,1,0:T(8,128)(2,1)S(1)} %slice.117) | copy-start | bytes 8257540
  117.2 2.9 copy-start.9
  117.6 6.2 %copy-start.8 = (bf16[32,48,896]{2,1,0:T(8,128)(2,1)}, bf16[32,48,896]{2,1,0:T(8,128)(2,1)S(1)}, u32[]{:S(2)}) copy-start(bf16[32,48,896]{2,1,0:T(8,128)(2,1)S(1)} %fusion.2) | copy-start | bytes 8257540
  130.0 2.5 copy-start.11
  158.8 185.0 %all-gather.7.cloned.1.call-start = ((), (), s32[]{:S(2)}) async-start(), calls=%async_computation.9 | async-start | bytes 11796480 | tf_op jit(solution)/shard_map/all_gather | solution.py:131
  365.8 3.0 copy-start.2
  369.5 6.3 %copy-start.3 = (bf16[1,1536,4,256]{1,3,2,0:T(8,128)(2,1)}, bf16[1,1536,4,256]{1,3,2,0:T(8,128)(2,1)S(1)}, u32[]{:S(2)}) copy-start(bf16[1,1536,4,256]{1,3,2,0:T(8,128)(2,1)S(1)} %copy.93) | copy-start | bytes 9437188
  369.5 2.9 copy-start.10
  370.1 5.6 %copy-start.5 = (bf16[1,1536,4,256]{1,3,2,0:T(8,128)(2,1)}, bf16[1,1536,4,256]{1,3,2,0:T(8,128)(2,1)S(1)}, u32[]{:S(2)}) copy-start(bf16[1,1536,4,256]{1,3,2,0:T(8,128)(2,1)S(1)} %copy.91) | copy-start | bytes 9437188
  372.3 3.4 copy-start.12
  389.9 82.4 %all-to-all-start.2 = ((bf16[32,48,1792]{2,1,0:T(8,128)(2,1)}), bf16[32,48,1792]{2,1,0:T(8,128)(2,1)}, u32[]{:S(2)}, u32[]{:S(2)}) async-start(bf16[32,48,1792]{2,1,0:T(8,128)(2,1)} %bitcast.99), calls=%async_computation.3 | async-start | bytes 11010048 | tf_op jit(solution)/shard_map/all_to_all | solution.py:137
  397.4 103.3 %reduce-scatter.7.cloned.1.call-start = ((), (), s32[]{:S(2)}) async-start(), calls=%async_computation.10 | async-start | bytes 81920 | tf_op jit(solution)/shard_map/reduce_scatter | solution.py:98
  398.5 7.5 %copy-start.4 = (bf16[1,1536,4,256]{1,3,2,0:T(8,128)(2,1)S(1)}, bf16[1,1536,4,256]{1,3,2,0:T(8,128)(2,1)}, u32[]{:S(2)}) copy-start(bf16[1,1536,4,256]{1,3,2,0:T(8,128)(2,1)} %copy-done.3) | copy-start | bytes 9437188
  398.5 7.5 %copy-start.7 = (bf16[32,48,896]{2,1,0:T(8,128)(2,1)S(1)}, bf16[32,48,896]{2,1,0:T(8,128)(2,1)}, u32[]{:S(2)}) copy-start(bf16[32,48,896]{2,1,0:T(8,128)(2,1)} %copy-done.6) | copy-start | bytes 8257540
  479.1 9.7 %all-to-all-start.4 = ((bf16[4,32,896]{2,1,0:T(8,128)(2,1)}), bf16[4,32,896]{2,1,0:T(8,128)(2,1)S(1)}, u32[]{:S(2)}, u32[]{:S(2)}) async-start(bf16[4,32,896]{2,1,0:T(8,128)(2,1)} %bitcast.25), calls=%async_computation.5 | async-start | bytes 458752 | tf_op jit(solution)/shard_map/all_to_all | solution.py:97
  488.8 14.3 %all-to-all-start.3 = ((bf16[4,32,896]{2,1,0:T(8,128)(2,1)}), bf16[4,32,896]{2,1,0:T(8,128)(2,1)S(1)}, u32[]{:S(2)}, u32[]{:S(2)}) async-start(bf16[4,32,896]{2,1,0:T(8,128)(2,1)} %bitcast.23), calls=%async_computation.4 | async-start | bytes 458752 | tf_op jit(solution)/shard_map/all_to_all | solution.py:96
  493.6 10.1 %copy-start.1 = (bf16[1,896,1024]{2,1,0:T(8,128)(2,1)S(1)}, bf16[1,896,1024]{2,1,0:T(8,128)(2,1)}, u32[]{:S(2)}) copy-start(bf16[1,896,1024]{2,1,0:T(8,128)(2,1)} %param.11) | copy-start | bytes 5505028
Sparse Core Ops, SparseCore 0:
  36.6 71.4 all-gather.4
  158.9 87.6 reduce-scatter.4
  250.9 92.8 all-gather.6
  476.1 15.6 reduce-scatter.6
where the time goes:
time: 521 us; the launch traced here: 511 us
  waiting for transfers between devices  317 us (61%)
  local copies, waits for them, and re-layouts  61.9 us (12%)
  matrix products  56.5 us (11%)
  starting transfers between devices  26.7 us (5%)
  other arithmetic  22.1 us (4%)
  between operations  14.4 us (3%)
  blocking collectives  11.9 us (2%)
    all_gather x1, waiting for transfers between devices, per_device(): terms = lax.all_gather(acts, 'dp', axis=0, tiled=False)  93 us
    reduce_scatter x1, waiting for transfers between devices, per_device(): pre = lax.psum_scatter(part, 'dp', scatter_dimension=0, tiled=True)  87.8 us
    all_gather x1, waiting for transfers between devices, dispatch(): lax.all_gather(jnp.concatenate([tok, grad, tab], axis=1), 'expert', axis=...  71.4 us
    all_to_all x1, waiting for transfers between devices, per_device(): lax.all_to_all(send, 'expert', split_axis=0, concat_axis=0, tiled=True)  61.9 us
    dot_general x11, matrix products, dot32(): return lax.dot_general(a, b, (dims, ((), ())), preferred_element_type=F32)  46.2 us
    unnamed x31, local copies, waits for them, and re-layouts  18.1 us
    reshape x1, local copies, waits for them, and re-layouts, per_device(): terms.reshape(n_dp, rows, 3, quarter).transpose(2, 1, 0, 3)  15.4 us
    all_gather x1, blocking collectives, dispatch(): tab = lax.all_gather(table, 'dp', axis=0, tiled=True)  11.9 us
  transfers between devices with their start and end apart: 9, of which 6 were waited for; matrix products, arithmetic and copies ran while one was open for 6% of the time, Pallas kernels for 0%

commit v1 on v0

--- a/solution.py
+++ b/solution.py
@@ -1,3 +1,4 @@
+import functools
 import jax
 import jax.numpy as jnp
 from jax import lax
@@ -6,6 +7,22 @@
 BF = jnp.bfloat16
 F32 = jnp.float32
 LANES = 128
+
+
+def _expand_ladders(values, device_axis):
+    piece_next = jnp.concatenate(
+        lax.all_to_all(
+            jnp.stack(jnp.split(values, lax.psum(1, device_axis), axis=1), 0),
+            device_axis,
+            split_axis=0,
+            concat_axis=0,
+        ),
+        axis=0,
+    )
+    return piece_next
+
+
+sums_all_update = functools.partial(_expand_ladders, device_axis="dp")
 
 
 def dot32(a, b, dims):
@@ -25,7 +42,7 @@
 
 def to_slices(array, n_dp):
     rows, width = array.shape
-    return lax.all_to_all(array, "dp", split_axis=1, concat_axis=0, tiled=True)
+    return sums_all_update(array)
 
 
 def dispatch(tokens, out_grad, table):

time: 521 us -> 521 us (level)
  no operation moved by 1% of the time
where the time goes in v1:
time: 521 us; the launch traced here: 510 us
  waiting for transfers between devices  317 us (61%)
  local copies, waits for them, and re-layouts  62.4 us (12%)
  matrix products  54.7 us (10%)
  starting transfers between devices  26.7 us (5%)
  other arithmetic  23.3 us (4%)
  between operations  14.4 us (3%)
  blocking collectives  11.9 us (2%)
    all_gather x1, waiting for transfers between devices, per_device(): terms = lax.all_gather(acts, 'dp', axis=0, tiled=False)  93 us
    reduce_scatter x1, waiting for transfers between devices, per_device(): pre = lax.psum_scatter(part, 'dp', scatter_dimension=0, tiled=True)  87.8 us
    all_gather x1, waiting for transfers between devices, dispatch(): lax.all_gather(jnp.concatenate([tok, grad, tab], axis=1), 'expert', axis=...  71.4 us
    all_to_all x1, waiting for transfers between devices, per_device(): lax.all_to_all(send, 'expert', split_axis=0, concat_axis=0, tiled=True)  61.9 us
    dot_general x11, matrix products, dot32(): return lax.dot_general(a, b, (dims, ((), ())), preferred_element_type=F32)  44.4 us
    unnamed x31, local copies, waits for them, and re-layouts  18.1 us
    reshape x1, local copies, waits for them, and re-layouts, per_device(): terms.reshape(n_dp, rows, 3, quarter).transpose(2, 1, 0, 3)  15.4 us
    all_gather x1, blocking collectives, dispatch(): tab = lax.all_gather(table, 'dp', axis=0, tiled=True)  11.9 us
  transfers between devices with their start and end apart: 9, of which 6 were waited for; matrix products, arithmetic and copies ran while one was open for 6% of the time, Pallas kernels for 0%

profile of v1, /device:TPU:34, one launch (start us, length us, event | category | flops | bytes accessed | tf_op | source)
XLA Modules:
  0.0 510.5 jit_solution(3451805264861443530)
XLA Ops:
  7.2 1.1 slice_bitcast_fusion.3
  8.2 0.7 pad_maximum_fusion.5
  9.0 4.8 all-to-all-start.1
  13.8 0.8 copy.61
  14.6 0.1 convert_reduce_fusion
  14.7 0.9 slice_bitcast_fusion.7
  15.7 0.7 pad_maximum_fusion.4
  16.4 0.8 copy.62
  17.2 0.1 fusion.32
  17.3 1.5 all-to-all-done.1
  18.8 4.8 all-to-all-start
  23.8 11.9 %all_gather.15 = bf16[128,128]{1,0:T(8,128)(2,1)S(1)} all-gather(bf16[32,128]{1,0:T(8,128)(2,1)S(1)} %pad_maximum_fusion.6), channel_id=1, replica_groups=mesh['dp'=4,'expert'=32] {'dp'}, dimensions={0}, use_global_device_ids=true | all-gather | bytes 40960 | tf_op jit(solution)/shard_map/all_gather | solution.py:52
  35.7 0.8 pad_maximum_fusion.3
  36.7 71.4 %all-gather.5.cloned.1.call-done = bf16[4096,1920]{1,0:T(8,128)(2,1)} async-done(((bf16[128,1920]{1,0:T(8,128)(2,1)}), bf16[4096,1920]{1,0:T(8,128)(2,1)}) %all-gather.5.cloned.1.call-update) | async-done | bytes 15728656 | tf_op jit(solution)/shard_map/all_gather | solution.py:53
  108.1 2.0 fusion.6
  110.1 6.4 %fusion = f32[32,48,1792]{2,1,0:T(8,128)S(1)} fusion(bf16[32,128,1920]{2,1,0:T(8,128)(2,1)} %bitcast.100, f32[32,128]{1,0:T(8,128)S(1)} %get-tuple-element.13, f32[48]{0:T(128)S(1)} %fusion.35, pred[48,128]{1,0:T(8,128)(4,1)S(1)} %broadcast_compare_fusion), kind=kOutput, calls=%fused_computation | convolution fusion | flops 705036288 | bytes 25712832 | tf_op jit(solution)/shard_map/dot_general | solution.py:68
  116.5 0.4 select_reduce_fusion
  116.9 0.3 slice.113
  117.2 0.4 fusion.2
  117.6 2.5 copy-done.9
  120.1 3.7 convolution_convert_fusion
  123.7 2.4 copy.67
  126.2 3.8 convolution_convert_fusion.2
  130.0 2.4 copy.65
  132.5 4.3 convolution_convert_fusion.1
  136.8 2.4 copy.66
  139.2 9.3 %pad_maximum_fusion = bf16[3,1536,4,256]{1,2,3,0:T(4,128)(2,1)} fusion(bf16[1,1536,4,256]{1,2,3,0:T(4,128)(2,1)S(1)} %copy.67, bf16[1,1536,4,256]{1,2,3,0:T(4,128)(2,1)S(1)} %copy.66, bf16[1,1536,4,256]{1,2,3,0:T(4,128)(2,1)S(1)} %copy.65), kind=kLoop, calls=%fused_computation.2 | loop fusion | flops 9437184 | bytes 18874368 | tf_op jit(solution)/shard_map/stack | solution.py:136
  148.5 10.4 %copy.80 = bf16[96,8,4,1536]{3,1,2,0:T(8,128)(2,1)} copy(bf16[96,8,4,1536]{3,2,1,0:T(4,128)(2,1)} %bitcast.103) | data formatting | bytes 18874368
  158.9 87.8 %reduce-scatter.5.cloned.1.call-done = bf16[1536,768]{0,1:T(8,128)(2,1)} async-done(((bf16[6144,768]{0,1:T(8,128)(2,1)}), bf16[1536,768]{0,1:T(8,128)(2,1)}) %reduce-scatter.5.cloned.1.call-update) | async-done | bytes 2359312 | tf_op jit(solution)/shard_map/reduce_scatter | solution.py:146
  246.7 2.6 fusion.14
  249.3 1.5 pad_maximum_fusion.2
  250.9 93.0 %all-gather.7.cloned.1.call-done = bf16[6144,768]{0,1:T(8,128)(2,1)} async-done(((bf16[1536,768]{0,1:T(8,128)(2,1)}), bf16[6144,768]{0,1:T(8,128)(2,1)}) %all-gather.7.cloned.1.call-update) | async-done | bytes 9437200 | tf_op jit(solution)/shard_map/all_gather | solution.py:148
  343.9 15.4 %reshape.278 = bf16[4,1536,3,256]{1,0,3,2:T(4,128)(2,1)} reshape(bf16[6144,768]{0,1:T(8,128)(2,1)} %all-gather.7.cloned.1.call-done) | data formatting | bytes 18874368 | tf_op jit(solution)/shard_map/reshape | solution.py:149
  359.3 6.1 %fusion.37 = (bf16[1,1536,4,256]{1,2,3,0:T(4,128)(2,1)S(1)}, bf16[1,1536,4,256]{1,2,3,0:T(4,128)(2,1)S(1)}, bf16[1,1536,4,256]{1,2,3,0:T(4,128)(2,1)S(1)}) fusion(bf16[3,1536,4,256]{1,2,3,0:T(4,128)(2,1)} %bitcast.102), kind=kLoop, calls=%fused_computation.99 | loop fusion | bytes 18874368 | tf_op jit(solution)/shard_map/slice | solution.py:150
  365.4 0.6 copy.69
  366.0 3.0 fusion.11
  369.0 0.6 copy.70
  369.6 0.6 copy.68
  370.2 2.3 copy-done.10
  372.5 3.3 convolution_convert_fusion.3
  375.9 3.3 add_convert_fusion
  379.1 2.8 pad_maximum_fusion.1
  381.9 7.9 %copy.71 = bf16[1536,1792]{1,0:T(8,128)(2,1)} copy(bf16[1536,1792]{0,1:T(8,128)(2,1)} %pad_maximum_fusion.1) | data formatting | bytes 11010048 | tf_op jit(solution)/shard_map/concatenate | solution.py:153
  389.8 7.5 %all-to-all-start.2 = ((bf16[32,48,1792]{2,1,0:T(8,128)(2,1)}), bf16[32,48,1792]{2,1,0:T(8,128)(2,1)}, u32[]{:S(2)}, u32[]{:S(2)}) async-start(bf16[32,48,1792]{2,1,0:T(8,128)(2,1)} %bitcast.104), calls=%async_computation.3 | async-start | bytes 11010048 | tf_op jit(solution)/shard_map/all_to_all | solution.py:154
  397.5 0.1 eq.122
  397.6 0.1 slice_add_fusion
  397.9 0.3 fusion.27
  398.2 0.3 bitcast_select_fusion
  398.5 7.5 %convert_bitcast_fusion = bf16[1,1024,896]{2,1,0:T(8,128)(2,1)} fusion(bf16[1536,1024]{0,1:T(8,128)(2,1)} %bitcast.110, bf16[1536,896]{1,0:T(8,128)(2,1)} %bitcast.119), kind=kOutput, calls=%fused_computation.32 | convolution fusion | flops 2819489792 | bytes 7733248 | tf_op jit(solution)/shard_map/dot_general | solution.py:29
  406.0 4.4 convert_bitcast_fusion.1
  410.4 61.9 %all-to-all-done.2 = bf16[32,48,1792]{2,1,0:T(8,128)(2,1)} async-done(((bf16[32,48,1792]{2,1,0:T(8,128)(2,1)}), bf16[32,48,1792]{2,1,0:T(8,128)(2,1)}, u32[]{:S(2)}, u32[]{:S(2)}) %all-to-all-start.2) | async-done | bytes 5505056 | tf_op jit(solution)/shard_map/all_to_all | solution.py:154
  472.3 2.0 slice.82
  474.3 0.9 fusion.23
  475.2 0.7 copy.76
  475.9 3.1 fusion.24
  479.0 4.5 all-to-all-start.4
  483.6 4.0 convolution_convert_fusion.4
  487.5 1.2 all-to-all-done.4
  488.7 4.9 all-to-all-start.3
  493.6 7.1 %convert_bitcast_fusion.2 = bf16[1,896,1024]{2,1,0:T(8,128)(2,1)} fusion(bf16[1536,896]{1,0:T(8,128)(2,1)} %bitcast.116, bf16[1536,1024]{0,1:T(8,128)(2,1)} %bitcast.106), kind=kOutput, calls=%fused_computation.34 | convolution fusion | flops 2819489792 | bytes 7733248 | tf_op jit(solution)/shard_map/dot_general | solution.py:29
  500.7 0.9 select_reduce_fusion.1
  501.6 0.7 copy.75
  502.3 0.7 copy.79
  503.0 0.7 copy.78
  (50 shorter events, 0.7 us)
Async XLA Ops:
  7.2 119.0 %copy-start = (bf16[1,896,1024]{2,1,0:T(8,128)(2,1)S(1)}, bf16[1,896,1024]{2,1,0:T(8,128)(2,1)}, u32[]{:S(2)}) copy-start(bf16[1,896,1024]{2,1,0:T(8,128)(2,1)} %param.11) | copy-start | bytes 5505028
  9.0 9.9 %all-to-all-start.1 = ((bf16[4,32,896]{2,1,0:T(8,128)(2,1)}), bf16[4,32,896]{2,1,0:T(8,128)(2,1)S(1)}, u32[]{:S(2)}, u32[]{:S(2)}) async-start(bf16[4,32,896]{2,1,0:T(8,128)(2,1)} %pad_maximum_fusion.5), calls=%async_computation.1 | async-start | bytes 458752 | tf_op jit(solution)/shard_map/all_to_all | solution.py:14
  18.8 16.8 %all-to-all-start = ((bf16[4,32,896]{2,1,0:T(8,128)(2,1)}), bf16[4,32,896]{2,1,0:T(8,128)(2,1)S(1)}, u32[]{:S(2)}, u32[]{:S(2)}) async-start(bf16[4,32,896]{2,1,0:T(8,128)(2,1)} %pad_maximum_fusion.4), calls=%async_computation | async-start | bytes 458752 | tf_op jit(solution)/shard_map/all_to_all | solution.py:14
  23.7 84.5 %all-gather.5.cloned.1.call-start = ((), (), s32[]{:S(2)}) async-start(), calls=%async_computation.8 | async-start | bytes 16220160 | tf_op jit(solution)/shard_map/all_gather | solution.py:53
  36.5 210.2 %reduce-scatter.5.cloned.1.call-start = ((), (), s32[]{:S(2)}) async-start(), calls=%async_computation.7 | async-start | bytes 11796480 | tf_op jit(solution)/shard_map/reduce_scatter | solution.py:146
  117.2 15.3 %copy-start.6 = (bf16[32,48,896]{2,1,0:T(8,128)(2,1)}, bf16[32,48,896]{2,1,0:T(8,128)(2,1)S(1)}, u32[]{:S(2)}) copy-start(bf16[32,48,896]{2,1,0:T(8,128)(2,1)S(1)} %slice.113) | copy-start | bytes 8257540
  117.2 2.9 copy-start.9
  117.6 6.2 %copy-start.8 = (bf16[32,48,896]{2,1,0:T(8,128)(2,1)}, bf16[32,48,896]{2,1,0:T(8,128)(2,1)S(1)}, u32[]{:S(2)}) copy-start(bf16[32,48,896]{2,1,0:T(8,128)(2,1)S(1)} %fusion.2) | copy-start | bytes 8257540
  130.0 2.5 copy-start.11
  158.8 185.1 %all-gather.7.cloned.1.call-start = ((), (), s32[]{:S(2)}) async-start(), calls=%async_computation.9 | async-start | bytes 11796480 | tf_op jit(solution)/shard_map/all_gather | solution.py:148
  366.0 3.0 copy-start.2
  369.6 6.3 %copy-start.3 = (bf16[1,1536,4,256]{1,3,2,0:T(8,128)(2,1)}, bf16[1,1536,4,256]{1,3,2,0:T(8,128)(2,1)S(1)}, u32[]{:S(2)}) copy-start(bf16[1,1536,4,256]{1,3,2,0:T(8,128)(2,1)S(1)} %copy.70) | copy-start | bytes 9437188
  369.6 2.9 copy-start.10
  370.2 5.6 %copy-start.5 = (bf16[1,1536,4,256]{1,3,2,0:T(8,128)(2,1)}, bf16[1,1536,4,256]{1,3,2,0:T(8,128)(2,1)S(1)}, u32[]{:S(2)}) copy-start(bf16[1,1536,4,256]{1,3,2,0:T(8,128)(2,1)S(1)} %copy.68) | copy-start | bytes 9437188
  372.5 3.4 copy-start.12
  389.8 82.4 %all-to-all-start.2 = ((bf16[32,48,1792]{2,1,0:T(8,128)(2,1)}), bf16[32,48,1792]{2,1,0:T(8,128)(2,1)}, u32[]{:S(2)}, u32[]{:S(2)}) async-start(bf16[32,48,1792]{2,1,0:T(8,128)(2,1)} %bitcast.104), calls=%async_computation.3 | async-start | bytes 11010048 | tf_op jit(solution)/shard_map/all_to_all | solution.py:154
  397.4 103.3 %reduce-scatter.7.cloned.1.call-start = ((), (), s32[]{:S(2)}) async-start(), calls=%async_computation.10 | async-start | bytes 81920 | tf_op jit(solution)/shard_map/reduce_scatter | solution.py:115
  398.5 7.5 %copy-start.4 = (bf16[1,1536,4,256]{1,3,2,0:T(8,128)(2,1)S(1)}, bf16[1,1536,4,256]{1,3,2,0:T(8,128)(2,1)}, u32[]{:S(2)}) copy-start(bf16[1,1536,4,256]{1,3,2,0:T(8,128)(2,1)} %copy-done.3) | copy-start | bytes 9437188
  398.5 7.5 %copy-start.7 = (bf16[32,48,896]{2,1,0:T(8,128)(2,1)S(1)}, bf16[32,48,896]{2,1,0:T(8,128)(2,1)}, u32[]{:S(2)}) copy-start(bf16[32,48,896]{2,1,0:T(8,128)(2,1)} %copy-done.6) | copy-start | bytes 8257540
  479.0 9.7 %all-to-all-start.4 = ((bf16[4,32,896]{2,1,0:T(8,128)(2,1)}), bf16[4,32,896]{2,1,0:T(8,128)(2,1)S(1)}, u32[]{:S(2)}, u32[]{:S(2)}) async-start(bf16[4,32,896]{2,1,0:T(8,128)(2,1)} %bitcast.31), calls=%async_computation.5 | async-start | bytes 458752 | tf_op jit(solution)/shard_map/all_to_all | solution.py:114
  488.7 14.3 %all-to-all-start.3 = ((bf16[4,32,896]{2,1,0:T(8,128)(2,1)}), bf16[4,32,896]{2,1,0:T(8,128)(2,1)S(1)}, u32[]{:S(2)}, u32[]{:S(2)}) async-start(bf16[4,32,896]{2,1,0:T(8,128)(2,1)} %bitcast.29), calls=%async_computation.4 | async-start | bytes 458752 | tf_op jit(solution)/shard_map/all_to_all | solution.py:113
  493.6 10.1 %copy-start.1 = (bf16[1,896,1024]{2,1,0:T(8,128)(2,1)S(1)}, bf16[1,896,1024]{2,1,0:T(8,128)(2,1)}, u32[]{:S(2)}) copy-start(bf16[1,896,1024]{2,1,0:T(8,128)(2,1)} %param.11) | copy-start | bytes 5505028
Sparse Core Ops, SparseCore 0:
  36.6 71.4 all-gather.4
  159.0 87.7 reduce-scatter.4
  251.0 92.8 all-gather.6
  476.1 15.6 reduce-scatter.6
